TPU v7x, 32 devices: a whole 2x2x4 slice. The times are simulated.
32 devices in a mesh: ops: 8 (over y, x, core), grp: 4 (over z).
Axes of the slice: x: 2, y: 2, z: 4, core: 2. Of those that a mesh axis runs over, the one named last changes fastest.
Arguments:
- wave: bfloat16 [32, 512, 512], P(None, 'ops'), may hold values from -12 to 12
- diag_energy: float32 [32, 512, 512], P(None, 'ops'), may hold values from 0.5 to 2
- left_ops: bfloat16 [32, 512, 512], P(('ops', 'grp')), may hold values from -0.1875 to 0.1875
- right_ops: bfloat16 [32, 512, 512], P(('ops', 'grp')), may hold values from -0.25 to 0.25
- pair_sectors: int32 [32, 2], replicated, may hold values from 0 to 31, all different within a row
- sector_slot: int32 [32], replicated, may hold values from 0 to 31, each once
Outputs:
- residual: float32 [32, 512, 512], P(None, 'ops', 'grp')
- sigma_out: float32 [32, 512, 512], P(None, 'ops', 'grp')
Inputs may be any that keep to these rules, and one draw needn't show every extreme that they name: `pair_sectors`: each row names two different sectors; every sector is named by some row. `sector_slot`: each slot once.
All inputs are finite; a program needn't handle non-finite values.
Results may differ from a plain program's by a relative error of at most 0.0062.
Values may be sent and summed in bfloat16 or wider, within the bound.
A program may use at most 64 MiB of HBM per device.

v0:
```python
import jax
import jax.numpy as jnp
from jax import lax
from jax.sharding import PartitionSpec as P


def segment_total(received, targets, sectors):
    choose = (targets[None, :] == jnp.arange(sectors, dtype=jnp.int32)[:, None]).astype(jnp.float32)
    return jnp.dot(
        choose, received, precision=lax.Precision.HIGHEST, preferred_element_type=jnp.float32
    )


def apply_pairs(vector, left_ops, right_ops, wanted):
    ops_count = lax.axis_size("ops")
    sectors, rows_here, block_width = vector.shape
    pair_dev = left_ops.shape[0]
    cell_count = rows_here * block_width
    outgoing = jnp.take(vector, wanted.reshape(-1), axis=0).reshape(
        ops_count, pair_dev * 2, rows_here, block_width
    )
    fetched = lax.all_to_all(outgoing, "ops", split_axis=0, concat_axis=2, tiled=True)
    inner_half = jnp.einsum(
        "pij,pjk->pik", left_ops, fetched[:, 0], preferred_element_type=jnp.float32
    ).astype(jnp.bfloat16)
    forward = jnp.einsum("pik,pkl->pil", inner_half, right_ops, preferred_element_type=jnp.float32)
    flipped = jnp.einsum(
        "pji,pjk->pik", left_ops, fetched[:, 1], preferred_element_type=jnp.float32
    ).astype(jnp.bfloat16)
    adjoint = jnp.einsum("pik,plk->pil", flipped, right_ops, preferred_element_type=jnp.float32)
    forward_parts = lax.all_to_all(
        forward.reshape(pair_dev, ops_count, rows_here, block_width),
        "ops",
        split_axis=1,
        concat_axis=1,
        tiled=True,
    )
    adjoint_parts = lax.all_to_all(
        adjoint.reshape(pair_dev, ops_count, rows_here, block_width),
        "ops",
        split_axis=1,
        concat_axis=1,
        tiled=True,
    )
    summed = segment_total(
        forward_parts.reshape(-1, cell_count), wanted[:, :, 1].T.reshape(-1), sectors
    )
    summed = summed + segment_total(
        adjoint_parts.reshape(-1, cell_count), wanted[:, :, 0].T.reshape(-1), sectors
    )
    return summed.reshape(sectors, rows_here, block_width)


def reduce_group(partial_value):
    return lax.psum_scatter(partial_value, "grp", scatter_dimension=2, tiled=True)


def body(wave, diag_energy, left_ops, right_ops, pair_sectors, sector_slot):
    ops_count = lax.axis_size("ops")
    grp_count = lax.axis_size("grp")
    pair_dev = left_ops.shape[0]
    block_width = wave.shape[2]
    stored = jnp.take(sector_slot, pair_sectors, axis=0).reshape(ops_count, grp_count, pair_dev, 2)
    wanted = lax.dynamic_index_in_dim(stored, lax.axis_index("grp"), 1, keepdims=False)
    column_share = block_width // grp_count
    column_start = lax.axis_index("grp") * column_share
    applied_sum = reduce_group(apply_pairs(wave, left_ops, right_ops, wanted))
    wave_wide = wave.astype(jnp.float32)
    diag_share = lax.dynamic_slice_in_dim(diag_energy, column_start, column_share, 2)
    wave_share = lax.dynamic_slice_in_dim(wave_wide, column_start, column_share, 2)
    applied = diag_share * wave_share + applied_sum
    products = lax.psum(
        (jnp.sum(wave_share * applied), jnp.sum(wave_share * wave_share)), ("ops", "grp")
    )
    rayleigh = products[0] / products[1]
    residual = applied - rayleigh * wave_share
    residual_half = residual.astype(jnp.bfloat16)
    full_half = lax.all_gather(residual_half, "grp", axis=2, tiled=True)
    second = reduce_group(apply_pairs(full_half, left_ops, right_ops, wanted))
    sigma_out = diag_share * residual_half.astype(jnp.float32) + second
    return (residual, sigma_out)


def solution(mesh):
    return jax.shard_map(
        body,
        mesh=mesh,
        in_specs=(
            P(None, "ops", None),
            P(None, "ops", None),
            P(("ops", "grp"), None, None),
            P(("ops", "grp"), None, None),
            P(),
            P(),
        ),
        out_specs=(P(None, "ops", "grp"), P(None, "ops", "grp")),
        check_vma=False,
    )
```

profile of v0, /device:TPU:9, one launch (start us, length us, event | category | flops | bytes accessed | tf_op | source)
XLA Modules:
  0.0 406.9 jit_solution(14706174111420252902)
XLA Ops:
  7.2 0.7 compare_select_fusion
  7.9 0.1 copy.44
  8.0 0.1 reshape.186
  8.2 0.8 gather_fusion
  8.9 0.1 reshape.185
  9.2 0.2 fusion.20
  9.4 0.1 copy.46
  9.7 2.2 gather_fusion.1
  11.9 0.2 broadcast_select_fusion.1
  12.1 18.3 %all_to_all.56 = bf16[8,2,64,512]{3,2,1,0:T(8,128)(2,1)S(1)} all-to-all(bf16[8,2,64,512]{3,2,1,0:T(8,128)(2,1)S(1)} %bitcast.115), channel_id=1, replica_groups=mesh['ops'=8,'grp'=4] {'ops'}, dimensions={0} | all-to-all | bytes 2097152 | tf_op jit(solution)/shard_map/all_to_all | solution.py:22
  30.4 0.1 copy.47
  30.5 0.5 convolution_convert_fusion.3
  31.0 1.4 convolution_bitcast_fusion.2
  32.4 4.7 %all-to-all-start.2 = ((f32[1,8,64,512]{3,2,0,1:T(8,128)}), f32[1,8,64,512]{3,2,0,1:T(8,128)S(1)}, u32[]{:S(2)}, u32[]{:S(2)}) async-start(f32[1,8,64,512]{3,2,0,1:T(8,128)} %convolution_bitcast_fusion.2), calls=%async_computation.2 | async-start | bytes 2097152 | tf_op jit(solution)/shard_map/all_to_all | solution.py:38
  37.1 0.4 convolution_convert_fusion.1
  37.6 1.4 convolution_bitcast_fusion.3
  39.0 10.1 %all-to-all-done.2 = f32[1,8,64,512]{3,2,0,1:T(8,128)S(1)} async-done(((f32[1,8,64,512]{3,2,0,1:T(8,128)}), f32[1,8,64,512]{3,2,0,1:T(8,128)S(1)}, u32[]{:S(2)}, u32[]{:S(2)}) %all-to-all-start.2) | async-done | bytes 1048608 | tf_op jit(solution)/shard_map/all_to_all | solution.py:38
  49.0 7.6 %all-to-all-start.1 = ((f32[1,8,64,512]{3,2,0,1:T(8,128)}), f32[1,8,64,512]{3,2,0,1:T(8,128)}, u32[]{:S(2)}, u32[]{:S(2)}) async-start(f32[1,8,64,512]{3,2,0,1:T(8,128)} %convolution_bitcast_fusion.3), calls=%async_computation.1 | async-start | bytes 2097152 | tf_op jit(solution)/shard_map/all_to_all | solution.py:31
  56.7 0.6 copy.54
  57.3 11.3 %all-to-all-done.1 = f32[1,8,64,512]{3,2,0,1:T(8,128)} async-done(((f32[1,8,64,512]{3,2,0,1:T(8,128)}), f32[1,8,64,512]{3,2,0,1:T(8,128)}, u32[]{:S(2)}, u32[]{:S(2)}) %all-to-all-start.1) | async-done | bytes 1048608 | tf_op jit(solution)/shard_map/all_to_all | solution.py:31
  68.6 1.8 copy.53
  70.4 1.8 fusion.13
  72.3 1.9 convolution_add_fusion.1
  74.2 4.4 %copy.55 = f32[4,8,64,512]{3,2,1,0:T(8,128)} copy(f32[4,8,64,512]{3,1,2,0:T(8,128)S(1)} %bitcast.109) | data formatting | bytes 8388608
  78.6 79.1 %reduce-scatter.3.cloned.1.call-done = f32[32,64,128]{2,1,0:T(8,128)} async-done(((f32[32,64,512]{2,1,0:T(8,128)}), f32[32,64,128]{2,1,0:T(8,128)}) %reduce-scatter.3.cloned.1.call-update) | async-done | bytes 1048592 | tf_op jit(solution)/shard_map/reduce_scatter | solution.py:55
  157.7 2.4 fusion.3
  160.2 39.3 %all-reduce = (f32[]{:T(128)}, f32[]{:T(128)}) all-reduce(f32[]{:T(128)} %get-tuple-element.4, f32[]{:T(128)} %get-tuple-element.3), channel_id=1, replica_groups=mesh['ops'=8,'grp'=4] {'ops','grp'}, use_global_device_ids=true, to_apply=%region_2.4 | all-reduce | flops 2 | bytes 16 | tf_op jit(solution)/shard_map/psum | solution.py:72
  200.8 3.1 fusion.18
  204.0 44.3 %all-gather.2.cloned.1.call-done = bf16[32,64,512]{2,1,0:T(8,128)(2,1)} async-done(((bf16[32,64,128]{2,1,0:T(8,128)(2,1)}), bf16[32,64,512]{2,1,0:T(8,128)(2,1)}) %all-gather.2.cloned.1.call-update) | async-done | bytes 2097168 | tf_op jit(solution)/shard_map/all_gather | solution.py:78
  248.3 2.2 gather_fusion.2
  250.5 0.2 broadcast_select_fusion
  250.6 19.2 %all_to_all.57 = bf16[8,2,64,512]{3,2,1,0:T(8,128)(2,1)S(1)} all-to-all(bf16[8,2,64,512]{3,2,1,0:T(8,128)(2,1)S(1)} %bitcast.114), channel_id=1, replica_groups=mesh['ops'=8,'grp'=4] {'ops'}, dimensions={0} | all-to-all | bytes 2097152 | tf_op jit(solution)/shard_map/all_to_all | solution.py:22
  269.9 0.1 copy.50
  269.9 0.5 convolution_convert_fusion.2
  270.4 1.4 convolution_bitcast_fusion
  271.9 4.7 %all-to-all-start.5 = ((f32[1,8,64,512]{3,2,0,1:T(8,128)}), f32[1,8,64,512]{3,2,0,1:T(8,128)S(1)}, u32[]{:S(2)}, u32[]{:S(2)}) async-start(f32[1,8,64,512]{3,2,0,1:T(8,128)} %convolution_bitcast_fusion), calls=%async_computation.6 | async-start | bytes 2097152 | tf_op jit(solution)/shard_map/all_to_all | solution.py:38
  276.6 0.4 convolution_convert_fusion
  277.0 1.4 convolution_bitcast_fusion.1
  278.4 10.1 %all-to-all-done.5 = f32[1,8,64,512]{3,2,0,1:T(8,128)S(1)} async-done(((f32[1,8,64,512]{3,2,0,1:T(8,128)}), f32[1,8,64,512]{3,2,0,1:T(8,128)S(1)}, u32[]{:S(2)}, u32[]{:S(2)}) %all-to-all-start.5) | async-done | bytes 1048608 | tf_op jit(solution)/shard_map/all_to_all | solution.py:38
  288.5 7.6 %all-to-all-start.4 = ((f32[1,8,64,512]{3,2,0,1:T(8,128)}), f32[1,8,64,512]{3,2,0,1:T(8,128)}, u32[]{:S(2)}, u32[]{:S(2)}) async-start(f32[1,8,64,512]{3,2,0,1:T(8,128)} %convolution_bitcast_fusion.1), calls=%async_computation.5 | async-start | bytes 2097152 | tf_op jit(solution)/shard_map/all_to_all | solution.py:31
  296.1 0.6 copy.57
  296.7 11.3 %all-to-all-done.4 = f32[1,8,64,512]{3,2,0,1:T(8,128)} async-done(((f32[1,8,64,512]{3,2,0,1:T(8,128)}), f32[1,8,64,512]{3,2,0,1:T(8,128)}, u32[]{:S(2)}, u32[]{:S(2)}) %all-to-all-start.4) | async-done | bytes 1048608 | tf_op jit(solution)/shard_map/all_to_all | solution.py:31
  308.0 1.8 copy.56
  309.8 1.8 fusion.12
  311.7 1.9 convolution_add_fusion
  313.6 4.4 %copy.58 = f32[4,8,64,512]{3,2,1,0:T(8,128)} copy(f32[4,8,64,512]{3,1,2,0:T(8,128)S(1)} %bitcast.108) | data formatting | bytes 8388608
  318.0 79.6 %reduce-scatter.5.cloned.1.call-done = f32[32,64,128]{2,1,0:T(8,128)} async-done(((f32[32,64,512]{2,1,0:T(8,128)}), f32[32,64,128]{2,1,0:T(8,128)}) %reduce-scatter.5.cloned.1.call-update) | async-done | bytes 1048592 | tf_op jit(solution)/shard_map/reduce_scatter | solution.py:55
  397.6 2.8 multiply_add_fusion
  (27 shorter events, 0.4 us)
Async XLA Ops:
  7.2 23.3 %copy-start = (bf16[1,512,512]{2,1,0:T(8,128)(2,1)S(1)}, bf16[1,512,512]{2,1,0:T(8,128)(2,1)}, u32[]{:S(2)}) copy-start(bf16[1,512,512]{2,1,0:T(8,128)(2,1)} %param.10) | copy-start | bytes 1572868
  7.2 1.0 copy-start.1
  8.2 1.0 copy-start.5
  11.9 19.1 %copy-start.2 = (bf16[1,512,512]{2,1,0:T(8,128)(2,1)S(1)}, bf16[1,512,512]{2,1,0:T(8,128)(2,1)}, u32[]{:S(2)}) copy-start(bf16[1,512,512]{2,1,0:T(8,128)(2,1)} %param.11) | copy-start | bytes 1572868
  32.4 16.6 %all-to-all-start.2 = ((f32[1,8,64,512]{3,2,0,1:T(8,128)}), f32[1,8,64,512]{3,2,0,1:T(8,128)S(1)}, u32[]{:S(2)}, u32[]{:S(2)}) async-start(f32[1,8,64,512]{3,2,0,1:T(8,128)} %convolution_bitcast_fusion.2), calls=%async_computation.2 | async-start | bytes 2097152 | tf_op jit(solution)/shard_map/all_to_all | solution.py:38
  49.0 19.5 %all-to-all-start.1 = ((f32[1,8,64,512]{3,2,0,1:T(8,128)}), f32[1,8,64,512]{3,2,0,1:T(8,128)}, u32[]{:S(2)}, u32[]{:S(2)}) async-start(f32[1,8,64,512]{3,2,0,1:T(8,128)} %convolution_bitcast_fusion.3), calls=%async_computation.1 | async-start | bytes 2097152 | tf_op jit(solution)/shard_map/all_to_all | solution.py:31
  56.7 101.0 %reduce-scatter.3.cloned.1.call-start = ((), (), s32[]{:S(2)}) async-start(), calls=%async_computation.8 | async-start | bytes 5242880 | tf_op jit(solution)/shard_map/reduce_scatter | solution.py:55
  78.6 79.2 %copy-start.4 = (bf16[32,64,512]{2,1,0:T(8,128)(2,1)S(1)}, bf16[32,64,512]{2,1,0:T(8,128)(2,1)}, u32[]{:S(2)}) copy-start(bf16[32,64,512]{2,1,0:T(8,128)(2,1)} %param.8) | copy-start | bytes 6291460
  78.6 169.7 %all-gather.2.cloned.1.call-start = ((), (), s32[]{:S(2)}) async-start(), calls=%async_computation.9 | async-start | bytes 2621440 | tf_op jit(solution)/shard_map/all_gather | solution.py:78
  271.9 16.6 %all-to-all-start.5 = ((f32[1,8,64,512]{3,2,0,1:T(8,128)}), f32[1,8,64,512]{3,2,0,1:T(8,128)S(1)}, u32[]{:S(2)}, u32[]{:S(2)}) async-start(f32[1,8,64,512]{3,2,0,1:T(8,128)} %convolution_bitcast_fusion), calls=%async_computation.6 | async-start | bytes 2097152 | tf_op jit(solution)/shard_map/all_to_all | solution.py:38
  288.5 19.5 %all-to-all-start.4 = ((f32[1,8,64,512]{3,2,0,1:T(8,128)}), f32[1,8,64,512]{3,2,0,1:T(8,128)}, u32[]{:S(2)}, u32[]{:S(2)}) async-start(f32[1,8,64,512]{3,2,0,1:T(8,128)} %convolution_bitcast_fusion.1), calls=%async_computation.5 | async-start | bytes 2097152 | tf_op jit(solution)/shard_map/all_to_all | solution.py:31
  296.1 101.5 %reduce-scatter.5.cloned.1.call-start = ((), (), s32[]{:S(2)}) async-start(), calls=%async_computation.10 | async-start | bytes 5242880 | tf_op jit(solution)/shard_map/reduce_scatter | solution.py:55
  318.0 79.6 %copy-start.3 = (bf16[32,64,128]{2,1,0:T(8,128)(2,1)S(1)}, bf16[32,64,128]{2,1,0:T(8,128)(2,1)}, u32[]{:S(2)}) copy-start(bf16[32,64,128]{2,1,0:T(8,128)(2,1)} %get-tuple-element.7) | copy-start | bytes 1572868
Sparse Core Ops, SparseCore 0:
  78.7 78.9 reduce-scatter.2
  204.1 44.1 all-gather.1
  318.1 79.3 reduce-scatter.4
where the time goes:
time: 409 us; the launch traced here: 407 us
  waiting for transfers between devices  246 us (60%)
  blocking collectives  76.8 us (19%)
  starting transfers between devices  24.7 us (6%)
  local copies, waits for them, and re-layouts  19.9 us (5%)
  between operations  15.3 us (4%)
  matrix products  15 us (4%)
  other arithmetic  9.45 us (2%)
    reduce_scatter x2, waiting for transfers between devices, reduce_group(): lax.psum_scatter(partial_value, 'grp', scatter_dimension=2, tiled=True)  159 us
    all_gather x1, waiting for transfers between devices, body(): full_half = lax.all_gather(residual_half, 'grp', axis=2, tiled=True)  44.3 us
    psum x1, blocking collectives, body(): lax.psum((jnp.sum(wave_share * applied), jnp.sum(wave_share * wave_share)...  39.3 us
    all_to_all x2, blocking collectives, apply_pairs(): lax.all_to_all(outgoing, 'ops', split_axis=0, concat_axis=2, tiled=True)  37.5 us
    all_to_all x2, waiting for transfers between devices, apply_pairs(): lax.all_to_all(forward.reshape(pair_dev, ops_count, rows_here, block_widt...  22.6 us
    all_to_all x2, waiting for transfers between devices, apply_pairs(): lax.all_to_all(adjoint.reshape(pair_dev, ops_count, rows_here, block_widt...  20.1 us
    all_to_all x2, starting transfers between devices, apply_pairs(): lax.all_to_all(forward.reshape(pair_dev, ops_count, rows_here, block_widt...  15.2 us
    unnamed x18, local copies, waits for them, and re-layouts  13.7 us
  transfers between devices with their start and end apart: 7, of which 7 were waited for; matrix products, arithmetic and copies ran while one was open for 1% of the time, Pallas kernels for 0%

commit v1 on v0

--- a/solution.py
+++ b/solution.py
@@ -1,7 +1,320 @@
+import functools
+
 import jax
 import jax.numpy as jnp
 from jax import lax
+from jax.experimental import pallas as pl
+from jax.experimental.pallas import tpu as pltpu
 from jax.sharding import PartitionSpec as P
+
+MESH = pl.DeviceIdType.MESH
+VMEM = pl.BlockSpec(memory_space=pltpu.VMEM)
+SMEM = pl.BlockSpec(memory_space=pltpu.SMEM)
+ANY = pl.BlockSpec(memory_space=pl.ANY)
+
+
+def peer_order(ops_count, grp_count):
+    far = sorted(range(grp_count), key=lambda s: -min(s, grp_count - s))
+    return [(do, dg) for dg in far for do in range(ops_count) if (do, dg) != (0, 0)]
+
+
+def greet(shifts, ops_count, grp_count):
+    o, g = lax.axis_index("ops"), lax.axis_index("grp")
+    barrier = pltpu.get_barrier_semaphore()
+    for do, dg in shifts:
+        there = (lax.rem(o + do, ops_count), lax.rem(g + dg, grp_count))
+        pl.semaphore_signal(barrier, inc=1, device_id=there, device_id_type=MESH)
+    pl.semaphore_wait(barrier, len(shifts))
+
+
+def fetch_kernel(ops_count, out_ref_rows, outgoing, blocks, send_sem, recv_sem, own_sem):
+    o, g = lax.axis_index("ops"), lax.axis_index("grp")
+    rows = out_ref_rows
+    shifts = [(do, 0) for do in range(1, ops_count)]
+    mine = blocks.at[:, pl.ds(pl.multiple_of(o * rows, rows), rows), :]
+    own = pltpu.make_async_copy(outgoing.at[o], mine, own_sem)
+    own.start()
+    greet(shifts, ops_count, lax.axis_size("grp"))
+    copies = []
+    for n, (do, _) in enumerate(shifts):
+        to = lax.rem(o + do, ops_count)
+        copy = pltpu.make_async_remote_copy(
+            src_ref=outgoing.at[to], dst_ref=mine,
+            send_sem=send_sem.at[n], recv_sem=recv_sem.at[n],
+            device_id=(to, g), device_id_type=MESH,
+        )
+        copy.start()
+        copies.append(copy)
+    own.wait()
+    for copy in copies:
+        copy.wait()
+
+
+def scatter_kernel(ops_count, grp_count, rows, cols, with_stats, *refs):
+    if with_stats:
+        blocks, stats, pieces, all_stats, send_sem, recv_sem, own_sem, ssend, srecv = refs
+    else:
+        blocks, pieces, send_sem, recv_sem, own_sem = refs
+    o, g = lax.axis_index("ops"), lax.axis_index("grp")
+    me = o * grp_count + g
+    shifts = peer_order(ops_count, grp_count)
+
+    def part(to_o, to_g):
+        return blocks.at[
+            :,
+            pl.ds(pl.multiple_of(to_o * rows, rows), rows),
+            pl.ds(pl.multiple_of(to_g * cols, cols), cols),
+        ]
+
+    waits = [pltpu.make_async_copy(part(o, g), pieces.at[me], own_sem.at[0])]
+    if with_stats:
+        waits.append(pltpu.make_async_copy(stats, all_stats.at[me], own_sem.at[1]))
+    for copy in waits:
+        copy.start()
+    greet(shifts, ops_count, grp_count)
+    for n, (do, dg) in enumerate(shifts):
+        there = (lax.rem(o + do, ops_count), lax.rem(g + dg, grp_count))
+        if with_stats:
+            copy = pltpu.make_async_remote_copy(
+                src_ref=stats, dst_ref=all_stats.at[me],
+                send_sem=ssend.at[n], recv_sem=srecv.at[n],
+                device_id=there, device_id_type=MESH,
+            )
+            copy.start()
+            waits.append(copy)
+        copy = pltpu.make_async_remote_copy(
+            src_ref=part(*there), dst_ref=pieces.at[me],
+            send_sem=send_sem.at[n], recv_sem=recv_sem.at[n],
+            device_id=there, device_id_type=MESH,
+        )
+        copy.start()
+        waits.append(copy)
+    for copy in waits:
+        copy.wait()
+
+
+def collect_kernel(ops_count, grp_count, rows, cols, pieces, blocks, send_sem, recv_sem, own_sem):
+    o, g = lax.axis_index("ops"), lax.axis_index("grp")
+    shifts = peer_order(ops_count, grp_count)
+    mine = blocks.at[
+        :,
+        pl.ds(pl.multiple_of(o * rows, rows), rows),
+        pl.ds(pl.multiple_of(g * cols, cols), cols),
+    ]
+    waits = [pltpu.make_async_copy(pieces.at[o * grp_count + g], mine, own_sem)]
+    waits[0].start()
+    greet(shifts, ops_count, grp_count)
+    for n, (do, dg) in enumerate(shifts):
+        to_o, to_g = lax.rem(o + do, ops_count), lax.rem(g + dg, grp_count)
+        copy = pltpu.make_async_remote_copy(
+            src_ref=pieces.at[to_o * grp_count + to_g], dst_ref=mine,
+            send_sem=send_sem.at[n], recv_sem=recv_sem.at[n],
+            device_id=(to_o, to_g), device_id_type=MESH,
+        )
+        copy.start()
+        waits.append(copy)
+    for copy in waits:
+        copy.wait()
+
+
+def slot_of(pair_ref, slot_ref, side, pair):
+    return slot_ref[pair_ref[side, pair]]
+
+
+def stage_kernel(ops_count, grp_count, pair_dev, pair_ref, slot_ref, wave, outgoing):
+    g = lax.axis_index("grp")
+    for to in range(ops_count):
+        for j in range(pair_dev):
+            pair = (to * grp_count + g) * pair_dev + j
+            for side in range(2):
+                outgoing[to, 2 * j + side] = wave[slot_of(pair_ref, slot_ref, side, pair)]
+
+
+def fold(value):
+    rows, width = value.shape
+    tall = jnp.sum(value.reshape(rows // 8, 8, width), axis=0)
+    total = tall[:, :128]
+    for c in range(1, width // 128):
+        total = total + tall[:, c * 128:(c + 1) * 128]
+    return total
+
+
+def pair_products(left, right, source, target):
+    inner = jnp.dot(left, source, preferred_element_type=jnp.float32).astype(jnp.bfloat16)
+    forward = jnp.dot(inner, right, preferred_element_type=jnp.float32)
+    flipped = lax.dot_general(
+        left, target, (((0,), (0,)), ((), ())), preferred_element_type=jnp.float32
+    ).astype(jnp.bfloat16)
+    adjoint = lax.dot_general(
+        flipped, right, (((1,), (1,)), ((), ())), preferred_element_type=jnp.float32
+    )
+    return forward, adjoint
+
+
+def pairs_kernel(pair_dev, with_stats, *refs):
+    if with_stats:
+        blocks, left, right, diag, wave, out, stats = refs
+        cross = jnp.zeros((8, 128), jnp.float32)
+    else:
+        blocks, left, right, out = refs
+    for j in range(pair_dev):
+        source, target = blocks[2 * j], blocks[2 * j + 1]
+        forward, adjoint = pair_products(left[j], right[j], source, target)
+        out[2 * j] = forward.astype(jnp.bfloat16)
+        out[2 * j + 1] = adjoint.astype(jnp.bfloat16)
+        if with_stats:
+            cross = cross + fold(target.astype(jnp.float32) * forward)
+            cross = cross + fold(source.astype(jnp.float32) * adjoint)
+    if with_stats:
+        zero = jnp.zeros((8, 128), jnp.float32)
+
+        def visit(k, carry):
+            top, norm = carry
+            v = wave[k].astype(jnp.float32)
+            square = v * v
+            return top + fold(diag[k] * square), norm + fold(square)
+
+        top, norm = lax.fori_loop(0, wave.shape[0], visit, (zero, zero))
+        stats[0] = top + cross
+        stats[1] = norm
+
+
+def add_pieces(pair_ref, slot_ref, pieces, total):
+    devices, held = pieces.shape[:2]
+    pair_dev = held // 2
+
+    def visit(d, carry):
+        for j in range(pair_dev):
+            pair = d * pair_dev + j
+            for side in range(2):
+                k = slot_of(pair_ref, slot_ref, 1 - side, pair)
+                total[k] = total[k] + pieces[d, 2 * j + side].astype(jnp.float32)
+        return carry
+
+    lax.fori_loop(0, devices, visit, 0)
+
+
+def residual_kernel(pair_ref, slot_ref, pieces, all_stats, diag, wave, residual, half, outgoing):
+    sectors = wave.shape[0]
+
+    def start(k, carry):
+        residual[k] = diag[k] * wave[k].astype(jnp.float32)
+        return carry
+
+    lax.fori_loop(0, sectors, start, 0)
+    add_pieces(pair_ref, slot_ref, pieces, residual)
+    sums = jnp.sum(all_stats[...], axis=0)
+    rayleigh = jnp.sum(sums[0]) / jnp.sum(sums[1])
+
+    def finish(k, carry):
+        value = residual[k] - rayleigh * wave[k].astype(jnp.float32)
+        residual[k] = value
+        half[k] = value.astype(jnp.bfloat16)
+        return carry
+
+    lax.fori_loop(0, sectors, finish, 0)
+    devices, held = outgoing.shape[:2]
+    pair_dev = held // 2
+
+    def hand_out(d, carry):
+        for j in range(pair_dev):
+            for side in range(2):
+                k = slot_of(pair_ref, slot_ref, side, d * pair_dev + j)
+                outgoing[d, 2 * j + side] = half[k]
+        return carry
+
+    lax.fori_loop(0, devices, hand_out, 0)
+
+
+def sigma_kernel(pair_ref, slot_ref, pieces, diag, half, sigma):
+    def start(k, carry):
+        sigma[k] = diag[k] * half[k].astype(jnp.float32)
+        return carry
+
+    lax.fori_loop(0, half.shape[0], start, 0)
+    add_pieces(pair_ref, slot_ref, pieces, sigma)
+
+
+def dma(count):
+    return pltpu.SemaphoreType.DMA((count,))
+
+
+def direct_body(wave, diag_energy, left_ops, right_ops, pair_sectors, sector_slot):
+    ops_count, grp_count = lax.axis_size("ops"), lax.axis_size("grp")
+    sectors, rows, width = wave.shape
+    height = rows * ops_count
+    pair_dev = left_ops.shape[0]
+    cols = width // grp_count
+    devices = ops_count * grp_count
+    peers = devices - 1
+    half_t, wide_t = jnp.bfloat16, jnp.float32
+    shape = jax.ShapeDtypeStruct
+    pair_sides = pair_sectors.T
+    start = lax.axis_index("grp") * cols
+    diag = lax.dynamic_slice_in_dim(diag_energy, start, cols, 2)
+    wave_share = lax.dynamic_slice_in_dim(wave, start, cols, 2)
+
+    outgoing = pl.pallas_call(
+        functools.partial(stage_kernel, ops_count, grp_count, pair_dev),
+        out_shape=shape((ops_count, 2 * pair_dev, rows, width), half_t),
+        in_specs=[SMEM, SMEM, VMEM], out_specs=VMEM, name="stage",
+    )(pair_sides, sector_slot, wave)
+    blocks = pl.pallas_call(
+        functools.partial(fetch_kernel, ops_count, rows),
+        out_shape=shape((2 * pair_dev, height, width), half_t),
+        in_specs=[ANY], out_specs=ANY, name="fetch",
+        scratch_shapes=[dma(ops_count - 1), dma(ops_count - 1), pltpu.SemaphoreType.DMA],
+        compiler_params=pltpu.CompilerParams(collective_id=0, has_side_effects=True),
+    )(outgoing)
+    partial_blocks, stats = pl.pallas_call(
+        functools.partial(pairs_kernel, pair_dev, True),
+        out_shape=(shape((2 * pair_dev, height, width), half_t), shape((2, 8, 128), wide_t)),
+        in_specs=[VMEM] * 5, out_specs=(VMEM, VMEM), name="pairs_first",
+    )(blocks, left_ops, right_ops, diag, wave_share)
+    pieces, all_stats = pl.pallas_call(
+        functools.partial(scatter_kernel, ops_count, grp_count, rows, cols, True),
+        out_shape=(
+            shape((devices, 2 * pair_dev, rows, cols), half_t),
+            shape((devices, 2, 8, 128), wide_t),
+        ),
+        in_specs=[ANY, ANY], out_specs=(ANY, ANY), name="scatter_first",
+        scratch_shapes=[dma(peers), dma(peers), dma(2), dma(peers), dma(peers)],
+        compiler_params=pltpu.CompilerParams(collective_id=1, has_side_effects=True),
+    )(partial_blocks, stats)
+    residual, residual_half, handed = pl.pallas_call(
+        residual_kernel,
+        out_shape=(
+            shape((sectors, rows, cols), wide_t),
+            shape((sectors, rows, cols), half_t),
+            shape((devices, 2 * pair_dev, rows, cols), half_t),
+        ),
+        in_specs=[SMEM, SMEM] + [VMEM] * 4, out_specs=(VMEM,) * 3, name="residual",
+    )(pair_sides, sector_slot, pieces, all_stats, diag, wave_share)
+    blocks = pl.pallas_call(
+        functools.partial(collect_kernel, ops_count, grp_count, rows, cols),
+        out_shape=shape((2 * pair_dev, height, width), half_t),
+        in_specs=[ANY], out_specs=ANY, name="collect",
+        scratch_shapes=[dma(peers), dma(peers), pltpu.SemaphoreType.DMA],
+        compiler_params=pltpu.CompilerParams(collective_id=2, has_side_effects=True),
+    )(handed)
+    partial_blocks = pl.pallas_call(
+        functools.partial(pairs_kernel, pair_dev, False),
+        out_shape=shape((2 * pair_dev, height, width), half_t),
+        in_specs=[VMEM] * 3, out_specs=VMEM, name="pairs_second",
+    )(blocks, left_ops, right_ops)
+    pieces = pl.pallas_call(
+        functools.partial(scatter_kernel, ops_count, grp_count, rows, cols, False),
+        out_shape=shape((devices, 2 * pair_dev, rows, cols), half_t),
+        in_specs=[ANY], out_specs=ANY, name="scatter_second",
+        scratch_shapes=[dma(peers), dma(peers), dma(1)],
+        compiler_params=pltpu.CompilerParams(collective_id=3, has_side_effects=True),
+    )(partial_blocks)
+    sigma_out = pl.pallas_call(
+        sigma_kernel,
+        out_shape=shape((sectors, rows, cols), wide_t),
+        in_specs=[SMEM, SMEM] + [VMEM] * 3, out_specs=VMEM, name="sigma",
+    )(pair_sides, sector_slot, pieces, diag, residual_half)
+    return residual, sigma_out
 
 
 def segment_total(received, targets, sectors):
@@ -55,7 +368,7 @@
     return lax.psum_scatter(partial_value, "grp", scatter_dimension=2, tiled=True)
 
 
-def body(wave, diag_energy, left_ops, right_ops, pair_sectors, sector_slot):
+def collective_body(wave, diag_energy, left_ops, right_ops, pair_sectors, sector_slot):
     ops_count = lax.axis_size("ops")
     grp_count = lax.axis_size("grp")
     pair_dev = left_ops.shape[0]
@@ -82,6 +395,14 @@
 
 
 def solution(mesh):
+    rows_tile, lane_tile, most_peers = 16, 128, 64
+
+    def body(wave, diag_energy, left_ops, right_ops, pair_sectors, sector_slot):
+        rows, width = wave.shape[1:]
+        fits = rows % rows_tile == 0 and width % (lane_tile * mesh.shape["grp"]) == 0
+        chosen = direct_body if fits and mesh.size <= most_peers else collective_body
+        return chosen(wave, diag_energy, left_ops, right_ops, pair_sectors, sector_slot)
+
     return jax.shard_map(
         body,
         mesh=mesh,

time: 409 us -> 131 us (0.32)
  waiting for transfers between devices: 246 us -> 0 us
  Pallas kernels: 0 us -> 126 us
  blocking collectives: 76.8 us -> 0 us
  starting transfers between devices: 24.7 us -> 0 us
  local copies, waits for them, and re-layouts: 19.9 us -> 4.19 us
  matrix products: 15 us -> 0 us
  between operations: 15.3 us -> 0.67 us
  other arithmetic: 9.45 us -> 0 us
    reduce_scatter x2 -> x0, waiting for transfers between devices: 159 us -> none  [reduce_group(): lax.psum_scatter(partial_value, 'grp', scatter_dimension=2, tiled=True)]
    pallas_call x0 -> x9, Pallas kernels: none -> 126 us  [the longest x2 62.9 us: direct_body(): pl.pallas_call(functools.partial(scatter_kernel, ops_count, grp_count, ro...]
    all_gather x1 -> x0, waiting for transfers between devices: 44.3 us -> none  [body(): full_half = lax.all_gather(residual_half, 'grp', axis=2, tiled=True)]
    all_to_all x4 -> x0, waiting for transfers between devices: 42.7 us -> none  [the longest x2 22.6 us: apply_pairs(): lax.all_to_all(forward.reshape(pair_dev, ops_count, rows_here, block_widt...]
    psum x1 -> x0, blocking collectives: 39.3 us -> none  [body(): lax.psum((jnp.sum(wave_share * applied), jnp.sum(wave_share * wave_share)...]
    all_to_all x2 -> x0, blocking collectives: 37.5 us -> none  [apply_pairs(): lax.all_to_all(outgoing, 'ops', split_axis=0, concat_axis=2, tiled=True)]
    all_to_all x4 -> x0, starting transfers between devices: 24.6 us -> none  [the longest x2 15.2 us: apply_pairs(): lax.all_to_all(forward.reshape(pair_dev, ops_count, rows_here, block_widt...]
    dot_general x12 -> x0, matrix products: 15 us -> none  [the longest x4 7.48 us: segment_total(): jnp.dot(choose, received, precision=lax.Precision.HIGHEST, preferred_elem...]
  transfers between devices with their start and end apart: 7 -> 0, of which waited for: 7 -> 0; matrix products, arithmetic and copies ran while one was open for 1% -> 0% of each run, Pallas kernels for 0% -> 0%
where the time goes in v1:
time: 131 us
  Pallas kernels  126 us (96%)
  local copies, waits for them, and re-layouts  4.19 us (3%)
    pallas_call x2, Pallas kernels, direct_body(): pl.pallas_call(functools.partial(scatter_kernel, ops_count, grp_count, ro...  62.9 us
    pallas_call x1, Pallas kernels, direct_body(): pl.pallas_call(functools.partial(collect_kernel, ops_count, grp_count, ro...  27.8 us
    pallas_call x1, Pallas kernels, direct_body(): pl.pallas_call(functools.partial(fetch_kernel, ops_count, rows), out_shap...  15.7 us
    pallas_call x1, Pallas kernels, direct_body(): pl.pallas_call(residual_kernel, out_shape=(shape((sectors, rows, cols), w...  4.98 us
    pallas_call x1, Pallas kernels, direct_body(): pl.pallas_call(functools.partial(pairs_kernel, pair_dev, True), out_shape...  4.67 us
    pallas_call x1, Pallas kernels, direct_body(): pl.pallas_call(functools.partial(pairs_kernel, pair_dev, False), out_shap...  3.75 us
    pallas_call x1, Pallas kernels, direct_body(): pl.pallas_call(sigma_kernel, out_shape=shape((sectors, rows, cols), wide_...  3.43 us
    pallas_call x1, Pallas kernels, direct_body(): pl.pallas_call(functools.partial(stage_kernel, ops_count, grp_count, pair...  2.65 us

profile of v1, /device:TPU:9, one launch (start us, length us, event | category | flops | bytes accessed | tf_op | source)
XLA Modules:
  0.0 130.7 jit_solution(5609400667941924450)
XLA Ops:
  0.6 1.9 %constant_dynamic-slice_fusion.refs_4_.wave = bf16[32,64,128]{2,1,0:T(8,128)(2,1)} fusion(bf16[32,64,512]{2,1,0:T(8,128)(2,1)} %wave.1, s32[]{:T(128)S(6)} %select_n.4), kind=kLoop, calls=%fused_computation | loop fusion | bytes 1048580 | tf_op jit(solution)/shard_map/dynamic_slice | solution.py:255
  2.5 2.3 %constant_dynamic-slice_fusion.1.refs_3_.diag = f32[32,64,128]{2,1,0:T(8,128)} fusion(f32[32,64,512]{2,1,0:T(8,128)} %param.7, s32[]{:T(128)S(6)} %select_n.4), kind=kLoop, calls=%fused_computation.1 | loop fusion | bytes 2097156 | tf_op jit(solution)/shard_map/dynamic_slice | solution.py:254
  4.8 2.7 %stage.1.outgoing = bf16[8,2,64,512]{3,2,1,0:T(8,128)(2,1)} custom-call(s32[2,32]{1,0:T(2,128)} %bitcast.1, s32[32]{0:T(128)} %slot_ref.5, bf16[32,64,512]{2,1,0:T(8,128)(2,1)} %wave.1), custom_call_target="tpu_custom_call" | custom-call | tf_op jit(solution)/shard_map/stage/pallas_call | solution.py:257
  7.5 15.7 %fetch.1.refs_0_ = bf16[2,512,512]{2,1,0:T(8,128)(2,1)} custom-call(bf16[8,2,64,512]{3,2,1,0:T(8,128)(2,1)} %stage.1.outgoing), custom_call_target="tpu_custom_call" | custom-call | tf_op jit(solution)/shard_map/fetch/pallas_call | solution.py:262
  23.2 4.7 %pairs_first.1 = (bf16[2,512,512]{2,1,0:T(8,128)(2,1)}, f32[2,8,128]{2,1,0:T(8,128)}) custom-call(bf16[2,512,512]{2,1,0:T(8,128)(2,1)} %fetch.1.refs_0_, bf16[1,512,512]{2,1,0:T(8,128)(2,1)} %refs_1_.3, bf16[1,512,512]{2,1,0:T(8,128)(2,1)} %refs_2_.3, f32[32,64,128]{2,1,0:T(8,128)} %constant_dynamic-slice_fusion.1.refs_3_.diag, ...), custom_call_target="tpu_custom_call" | custom-call | tf_op jit(solution)/shard_map/pairs_first/pallas_call | solution.py:269
  27.8 35.0 %scatter_first.1 = (bf16[32,2,64,128]{3,2,1,0:T(8,128)(2,1)}, f32[32,2,8,128]{3,2,1,0:T(8,128)}) custom-call(bf16[2,512,512]{2,1,0:T(8,128)(2,1)} %get-tuple-element.9.refs_0_, f32[2,8,128]{2,1,0:T(8,128)} %get-tuple-element.10.refs_1_), custom_call_target="tpu_custom_call" | custom-call | tf_op jit(solution)/shard_map/scatter_first/pallas_call | solution.py:274
  62.9 5.0 %residual.1 = (f32[32,64,128]{2,1,0:T(8,128)}, bf16[32,64,128]{2,1,0:T(8,128)(2,1)}, bf16[32,2,64,128]{3,2,1,0:T(8,128)(2,1)}) custom-call(s32[2,32]{1,0:T(2,128)} %bitcast.2, s32[32]{0:T(128)} %slot_ref.5, bf16[32,2,64,128]{3,2,1,0:T(8,128)(2,1)} %get-tuple-element.11.pieces, f32[32,2,8,128]{3,2,1,0:T(8,128)} %get-tuple-element.12.all_stats, ...), custom_call_target="tpu_custom_call" | custom-call | tf_op jit(solution)/shard_map/residual/pallas_call | solution.py:284
  67.9 27.8 %collect.1.refs_0_ = bf16[2,512,512]{2,1,0:T(8,128)(2,1)} custom-call(bf16[32,2,64,128]{3,2,1,0:T(8,128)(2,1)} %get-tuple-element.14.pieces), custom_call_target="tpu_custom_call" | custom-call | tf_op jit(solution)/shard_map/collect/pallas_call | solution.py:293
  95.6 3.8 %pairs_second.1.refs_0_ = bf16[2,512,512]{2,1,0:T(8,128)(2,1)} custom-call(bf16[2,512,512]{2,1,0:T(8,128)(2,1)} %collect.1.refs_0_, bf16[1,512,512]{2,1,0:T(8,128)(2,1)} %refs_1_.3, bf16[1,512,512]{2,1,0:T(8,128)(2,1)} %refs_2_.3), custom_call_target="tpu_custom_call" | custom-call | tf_op jit(solution)/shard_map/pairs_second/pallas_call | solution.py:300
  99.4 27.9 %scatter_second.1.pieces = bf16[32,2,64,128]{3,2,1,0:T(8,128)(2,1)} custom-call(bf16[2,512,512]{2,1,0:T(8,128)(2,1)} %pairs_second.1.refs_0_), custom_call_target="tpu_custom_call" | custom-call | tf_op jit(solution)/shard_map/scatter_second/pallas_call | solution.py:305
  127.3 3.4 %sigma.1 = f32[32,64,128]{2,1,0:T(8,128)} custom-call(s32[2,32]{1,0:T(2,128)} %bitcast.3, s32[32]{0:T(128)} %slot_ref.5, bf16[32,2,64,128]{3,2,1,0:T(8,128)(2,1)} %scatter_second.1.pieces, f32[32,64,128]{2,1,0:T(8,128)} %constant_dynamic-slice_fusion.1.refs_3_.diag, bf16[32,64,128]{2,1,0:T(8,128)(2,1)} %get-tuple-element.15.half), custom_call_target="tpu_custom_call" | custom-call | tf_op jit(solution)/shard_map/sigma/pallas_call | solution.py:312

commit v2 on v0

--- a/solution.py
+++ b/solution.py
@@ -1,7 +1,334 @@
+import functools
+
 import jax
 import jax.numpy as jnp
 from jax import lax
+from jax.experimental import pallas as pl
+from jax.experimental.pallas import tpu as pltpu
 from jax.sharding import PartitionSpec as P
+
+MESH = pl.DeviceIdType.MESH
+VMEM = pl.BlockSpec(memory_space=pltpu.VMEM)
+SMEM = pl.BlockSpec(memory_space=pltpu.SMEM)
+ANY = pl.BlockSpec(memory_space=pl.ANY)
+
+
+def chain_kernel(pair_sides, sector_slot, slots, previous, keep, last):
+    pairs = pair_sides.shape[1]
+    sectors = sector_slot.shape[0]
+
+    def clear(k, carry):
+        last[k] = -1
+        return carry
+
+    lax.fori_loop(0, sectors, clear, 0)
+    for side in range(2):
+
+        def visit(p, carry, side=side):
+            item = side * pairs + p
+            slots[item] = sector_slot[pair_sides[side, p]]
+            k = sector_slot[pair_sides[1 - side, p]]
+            before = last[k]
+            previous[item] = jnp.maximum(before, 0)
+            keep[item] = jnp.where(before >= 0, 1.0, 0.0)
+            last[k] = item
+            return carry
+
+        lax.fori_loop(0, pairs, visit, 0)
+
+
+def fold(value):
+    rows, width = value.shape
+    tall = jnp.sum(value.reshape(rows // 8, 8, width), axis=0)
+    total = tall[:, :128]
+    for c in range(1, width // 128):
+        total = total + tall[:, c * 128:(c + 1) * 128]
+    return total
+
+
+def product(side, left, right, block):
+    half = lax.dot_general(
+        left, block, (((1 - side,), (0,)), ((), ())), preferred_element_type=jnp.float32
+    ).astype(jnp.bfloat16)
+    return lax.dot_general(
+        half, right, (((1,), (side,)), ((), ())), preferred_element_type=jnp.float32
+    )
+
+
+def whole_kernel(
+    ops_count, grp_count, pair_dev,
+    slots, previous, keep, last, wave_in, diag_in, left_in, right_in,
+    residual_out, sigma_out,
+    wave, diag, left, right, send_a, blocks_a, out_b, pieces_b, send_c, blocks_c,
+    out_d, pieces_d, run, residual, half, sigma, stats, all_stats,
+    load_sem, own_sem, send_sem, recv_sem,
+):
+    o, g = lax.axis_index("ops"), lax.axis_index("grp")
+    me = o * grp_count + g
+    devices = ops_count * grp_count
+    pairs = devices * pair_dev
+    sectors, rows, width = wave.shape
+    cols = width // grp_count
+    wide = jnp.float32
+    far_first = sorted(range(grp_count), key=lambda s: -min(s, grp_count - s))
+    my_cols = pl.ds(pl.multiple_of(g * cols, cols), cols)
+
+    def each_peer(visit):
+        for dg in far_first:
+
+            def step(do, carry, dg=dg):
+                visit(lax.rem(o + do, ops_count), lax.rem(g + dg, grp_count))
+                return carry
+
+            lax.fori_loop(1 if dg == 0 else 0, ops_count, step, 0)
+
+    def place(ref, side, at_o, at_g):
+        return ref.at[
+            side, :,
+            pl.ds(pl.multiple_of(at_o * rows, rows), rows),
+            pl.ds(pl.multiple_of(at_g * cols, cols), cols),
+        ]
+
+    def send(group, source, target, to_o, to_g):
+        pltpu.make_async_remote_copy(
+            src_ref=source, dst_ref=target,
+            send_sem=send_sem.at[group], recv_sem=recv_sem.at[group],
+            device_id=(to_o, to_g), device_id_type=MESH,
+        ).start()
+
+    def whole_of(group, like):
+        return pltpu.make_async_remote_copy(
+            src_ref=like, dst_ref=like,
+            send_sem=send_sem.at[group], recv_sem=recv_sem.at[group],
+            device_id=(lax.rem(o + 1, ops_count), g), device_id_type=MESH,
+        )
+
+    loads = [
+        pltpu.make_async_copy(wave_in, wave, load_sem.at[0]),
+        pltpu.make_async_copy(left_in, left, load_sem.at[1]),
+        pltpu.make_async_copy(right_in, right, load_sem.at[2]),
+        pltpu.make_async_copy(diag_in.at[:, :, my_cols], diag, load_sem.at[3]),
+    ]
+    for load in loads:
+        load.start()
+    barrier = pltpu.get_barrier_semaphore()
+    each_peer(
+        lambda to_o, to_g: pl.semaphore_signal(
+            barrier, inc=1, device_id=(to_o, to_g), device_id_type=MESH
+        )
+    )
+
+    loads[0].wait()
+
+    def stage(side):
+        for to in range(ops_count):
+            for j in range(pair_dev):
+                pair = (to * grp_count + g) * pair_dev + j
+                send_a[side, to, j] = wave[slots[side * pairs + pair]]
+
+    fetch_groups, own = (0, 1), []
+    stage(0)
+    pl.semaphore_wait(barrier, devices - 1)
+    my_rows = pl.ds(pl.multiple_of(o * rows, rows), rows)
+    for side in range(2):
+        if side == 1:
+            stage(1)
+
+        def fetch(do, carry, side=side):
+            to = lax.rem(o + do, ops_count)
+            send(fetch_groups[side], send_a.at[side, to], blocks_a.at[side, :, my_rows, :], to, g)
+            return carry
+
+        lax.fori_loop(1, ops_count, fetch, 0)
+        own.append(
+            pltpu.make_async_copy(
+                send_a.at[side, o], blocks_a.at[side, :, my_rows, :], own_sem.at[side]
+            )
+        )
+        own[side].start()
+
+    loads[3].wait()
+    zero = jnp.zeros((8, 128), wide)
+
+    def tally(k, carry):
+        value = wave[k, :, my_cols].astype(wide)
+        square = value * value
+        return carry[0] + fold(diag[k] * square), carry[1] + fold(square)
+
+    top, norm = lax.fori_loop(0, sectors, tally, (zero, zero))
+    loads[1].wait()
+    loads[2].wait()
+
+    def arrive(group, like):
+        whole_of(group, like).wait_recv()
+
+    def leave(group, like):
+        whole_of(group, like).wait_send()
+
+    fetch_like = [blocks_a.at[s, :, pl.ds(0, (ops_count - 1) * rows), :] for s in range(2)]
+    like_b = [pieces_b.at[s, pl.ds(0, (devices - 1) * pair_dev)] for s in range(2)]
+    like_c = [send_c.at[s, pl.ds(0, (devices - 1) * pair_dev)] for s in range(2)]
+    like_d = [pieces_d.at[s, pl.ds(0, (devices - 1) * pair_dev)] for s in range(2)]
+    stats_like = all_stats.at[pl.ds(0, devices - 1)]
+    my_pairs = pl.ds(me * pair_dev, pair_dev)
+
+    def scatter(side, group, out, pieces):
+        copy = pltpu.make_async_copy(
+            place(out, side, o, g), pieces.at[side, my_pairs], own_sem.at[group]
+        )
+        copy.start()
+        each_peer(
+            lambda to_o, to_g: send(
+                group, place(out, side, to_o, to_g), pieces.at[side, my_pairs], to_o, to_g
+            )
+        )
+        return copy
+
+    for side in range(2):
+        arrive(fetch_groups[side], fetch_like[side])
+        own[side].wait()
+        if side == 1:
+            for j in range(pair_dev):
+                value = product(1, left[j], right[j], blocks_a[1, j])
+                out_b[1, j] = value.astype(jnp.bfloat16)
+                top = top + fold(blocks_a[0, j].astype(wide) * value)
+                top = top + fold(blocks_a[1, j].astype(wide) * out_f[j])
+            stats[0] = top
+            stats[1] = norm
+            own.append(pltpu.make_async_copy(stats, all_stats.at[me], own_sem.at[8]))
+            own[-1].start()
+            each_peer(lambda to_o, to_g: send(8, stats, all_stats.at[me], to_o, to_g))
+        else:
+            out_f = []
+            for j in range(pair_dev):
+                value = product(0, left[j], right[j], blocks_a[0, j])
+                out_b[0, j] = value.astype(jnp.bfloat16)
+                out_f.append(value)
+        own.append(scatter(side, 2 + side, out_b, pieces_b))
+
+    def chain(pieces):
+        for side in range(2):
+
+            def visit(p, carry, side=side):
+                item = side * pairs + p
+                run[item] = pieces[side, p].astype(wide) + keep[item] * run[previous[item]]
+                return carry
+
+            lax.fori_loop(0, pairs, visit, 0)
+
+    for copy in own[2:]:
+        copy.wait()
+    for side in range(2):
+        arrive(2 + side, like_b[side])
+    arrive(8, stats_like)
+    run[0] = jnp.zeros((rows, cols), wide)
+    chain(pieces_b)
+    sums = jnp.sum(all_stats[...], axis=0)
+    rayleigh = jnp.sum(sums[0]) / jnp.sum(sums[1])
+
+    def finish(k, carry):
+        value = (diag[k] - rayleigh) * wave[k, :, my_cols].astype(wide) + run[last[k]]
+        residual[k] = value
+        half[k] = value.astype(jnp.bfloat16)
+        return carry
+
+    lax.fori_loop(0, sectors, finish, 0)
+    residual_copy = pltpu.make_async_copy(residual, residual_out, load_sem.at[0])
+    residual_copy.start()
+
+    own = []
+    for side in range(2):
+
+        def hand_out(p, carry, side=side):
+            send_c[side, p] = half[slots[side * pairs + p]]
+            return carry
+
+        lax.fori_loop(0, pairs, hand_out, 0)
+
+        def collect(to_o, to_g, side=side):
+            to = to_o * grp_count + to_g
+            source = send_c.at[side, pl.ds(to * pair_dev, pair_dev)]
+            send(4 + side, source, place(blocks_c, side, o, g), to_o, to_g)
+
+        each_peer(collect)
+        own.append(
+            pltpu.make_async_copy(
+                send_c.at[side, my_pairs], place(blocks_c, side, o, g), own_sem.at[4 + side]
+            )
+        )
+        own[side].start()
+    for side in range(2):
+        own[side].wait()
+        arrive(4 + side, like_c[side])
+        for j in range(pair_dev):
+            value = product(side, left[j], right[j], blocks_c[side, j])
+            out_d[side, j] = value.astype(jnp.bfloat16)
+        own.append(scatter(side, 6 + side, out_d, pieces_d))
+    for side in range(2):
+        own[2 + side].wait()
+        arrive(6 + side, like_d[side])
+    run[0] = jnp.zeros((rows, cols), wide)
+    chain(pieces_d)
+
+    def close(k, carry):
+        sigma[k] = diag[k] * half[k].astype(wide) + run[last[k]]
+        return carry
+
+    lax.fori_loop(0, sectors, close, 0)
+    sigma_copy = pltpu.make_async_copy(sigma, sigma_out, load_sem.at[1])
+    sigma_copy.start()
+    for side in range(2):
+        leave(side, fetch_like[side])
+        leave(2 + side, like_b[side])
+        leave(4 + side, like_c[side])
+        leave(6 + side, like_d[side])
+    leave(8, stats_like)
+    residual_copy.wait()
+    sigma_copy.wait()
+
+
+def direct_body(wave, diag_energy, left_ops, right_ops, pair_sectors, sector_slot):
+    ops_count, grp_count = lax.axis_size("ops"), lax.axis_size("grp")
+    sectors, rows, width = wave.shape
+    height = rows * ops_count
+    pair_dev = left_ops.shape[0]
+    pairs = pair_sectors.shape[0]
+    cols = width // grp_count
+    devices = ops_count * grp_count
+    thin, wide = jnp.bfloat16, jnp.float32
+    shape = jax.ShapeDtypeStruct
+    chains = pl.pallas_call(
+        chain_kernel,
+        out_shape=(
+            shape((2 * pairs,), jnp.int32), shape((2 * pairs,), jnp.int32),
+            shape((2 * pairs,), wide), shape((sectors,), jnp.int32),
+        ),
+        in_specs=[SMEM, SMEM], out_specs=(SMEM,) * 4, name="chain",
+    )(pair_sectors.T, sector_slot)
+    blocks = (2, pair_dev, height, width)
+    pieces = (2, pairs, rows, cols)
+    share = (sectors, rows, cols)
+    return pl.pallas_call(
+        functools.partial(whole_kernel, ops_count, grp_count, pair_dev),
+        out_shape=(shape(share, wide), shape(share, wide)),
+        in_specs=[SMEM] * 4 + [ANY] * 4, out_specs=(ANY, ANY), name="whole",
+        scratch_shapes=[
+            pltpu.VMEM(wave.shape, thin), pltpu.VMEM(share, wide),
+            pltpu.VMEM(left_ops.shape, thin), pltpu.VMEM(right_ops.shape, thin),
+            pltpu.VMEM((2, ops_count, pair_dev, rows, width), thin), pltpu.VMEM(blocks, thin),
+            pltpu.VMEM(blocks, thin), pltpu.VMEM(pieces, thin),
+            pltpu.VMEM(pieces, thin), pltpu.VMEM(blocks, thin),
+            pltpu.VMEM(blocks, thin), pltpu.VMEM(pieces, thin),
+            pltpu.VMEM((2 * pairs, rows, cols), wide), pltpu.VMEM(share, wide),
+            pltpu.VMEM(share, thin), pltpu.VMEM(share, wide),
+            pltpu.VMEM((2, 8, 128), wide), pltpu.VMEM((devices, 2, 8, 128), wide),
+            pltpu.SemaphoreType.DMA((4,)), pltpu.SemaphoreType.DMA((9,)),
+            pltpu.SemaphoreType.DMA((9,)), pltpu.SemaphoreType.DMA((9,)),
+        ],
+        compiler_params=pltpu.CompilerParams(
+            collective_id=0, has_side_effects=True, vmem_limit_bytes=48 << 20
+        ),
+    )(*chains, wave, diag_energy, left_ops, right_ops)
 
 
 def segment_total(received, targets, sectors):
@@ -55,7 +382,7 @@
     return lax.psum_scatter(partial_value, "grp", scatter_dimension=2, tiled=True)
 
 
-def body(wave, diag_energy, left_ops, right_ops, pair_sectors, sector_slot):
+def collective_body(wave, diag_energy, left_ops, right_ops, pair_sectors, sector_slot):
     ops_count = lax.axis_size("ops")
     grp_count = lax.axis_size("grp")
     pair_dev = left_ops.shape[0]
@@ -82,6 +409,14 @@
 
 
 def solution(mesh):
+    rows_tile, lane_tile, most_peers = 16, 128, 64
+
+    def body(wave, diag_energy, left_ops, right_ops, pair_sectors, sector_slot):
+        rows, width = wave.shape[1:]
+        fits = rows % rows_tile == 0 and width % (lane_tile * mesh.shape["grp"]) == 0
+        chosen = direct_body if fits and mesh.size <= most_peers else collective_body
+        return chosen(wave, diag_energy, left_ops, right_ops, pair_sectors, sector_slot)
+
     return jax.shard_map(
         body,
         mesh=mesh,

time: 409 us -> 104 us (0.25)
  waiting for transfers between devices: 246 us -> 0 us
  Pallas kernels: 0 us -> 95 us
  blocking collectives: 76.8 us -> 0 us
  starting transfers between devices: 24.7 us -> 0 us
  matrix products: 15 us -> 0 us
  between operations: 15.3 us -> 0.66 us
  local copies, waits for them, and re-layouts: 19.9 us -> 8.24 us
  other arithmetic: 9.45 us -> 0 us
    reduce_scatter x2 -> x0, waiting for transfers between devices: 159 us -> none  [reduce_group(): lax.psum_scatter(partial_value, 'grp', scatter_dimension=2, tiled=True)]
    pallas_call x0 -> x2, Pallas kernels: none -> 95 us  [the longest x1 92.7 us: direct_body(): pl.pallas_call(functools.partial(whole_kernel, ops_count, grp_count, pair...]
    all_gather x1 -> x0, waiting for transfers between devices: 44.3 us -> none  [body(): full_half = lax.all_gather(residual_half, 'grp', axis=2, tiled=True)]
    all_to_all x4 -> x0, waiting for transfers between devices: 42.7 us -> none  [the longest x2 22.6 us: apply_pairs(): lax.all_to_all(forward.reshape(pair_dev, ops_count, rows_here, block_widt...]
    psum x1 -> x0, blocking collectives: 39.3 us -> none  [body(): lax.psum((jnp.sum(wave_share * applied), jnp.sum(wave_share * wave_share)...]
    all_to_all x2 -> x0, blocking collectives: 37.5 us -> none  [apply_pairs(): lax.all_to_all(outgoing, 'ops', split_axis=0, concat_axis=2, tiled=True)]
    all_to_all x4 -> x0, starting transfers between devices: 24.6 us -> none  [the longest x2 15.2 us: apply_pairs(): lax.all_to_all(forward.reshape(pair_dev, ops_count, rows_here, block_widt...]
    dot_general x12 -> x0, matrix products: 15 us -> none  [the longest x4 7.48 us: segment_total(): jnp.dot(choose, received, precision=lax.Precision.HIGHEST, preferred_elem...]
  transfers between devices with their start and end apart: 7 -> 0, of which waited for: 7 -> 0; matrix products, arithmetic and copies ran while one was open for 1% -> 0% of each run, Pallas kernels for 0% -> 0%
where the time goes in v2:
time: 104 us
  Pallas kernels  95 us (91%)
  local copies, waits for them, and re-layouts  8.24 us (8%)
    pallas_call x1, Pallas kernels, direct_body(): pl.pallas_call(functools.partial(whole_kernel, ops_count, grp_count, pair...  92.7 us
    unnamed x16, local copies, waits for them, and re-layouts  8.24 us
    pallas_call x1, Pallas kernels, direct_body(): pl.pallas_call(chain_kernel, out_shape=(shape((2 * pairs,), jnp.int32), s...  2.34 us

profile of v2, /device:TPU:9, one launch (start us, length us, event | category | flops | bytes accessed | tf_op | source)
XLA Modules:
  0.0 103.9 jit_solution(15402578837864304055)
XLA Ops:
  0.6 2.3 %chain.1 = (s32[64]{0:T(128)}, s32[64]{0:T(128)}, f32[64]{0:T(128)}, s32[32]{0:T(128)}) custom-call(s32[2,32]{1,0:T(2,128)} %bitcast.1, s32[32]{0:T(128)} %sector_slot.1), custom_call_target="tpu_custom_call" | custom-call | tf_op jit(solution)/shard_map/chain/pallas_call | solution.py:300
  3.0 0.0 copy-start
  3.0 1.6 %copy-done = bf16[32,64,512]{2,1,0:T(8,128)(2,1)S(1)} copy-done((bf16[32,64,512]{2,1,0:T(8,128)(2,1)S(1)}, bf16[32,64,512]{2,1,0:T(8,128)(2,1)}, u32[]{:S(2)}) %copy-start) | copy-done | bytes 2097176
  4.6 0.0 copy-start.1
  4.6 1.0 %copy-done.1 = bf16[1,512,512]{2,1,0:T(8,128)(2,1)S(1)} copy-done((bf16[1,512,512]{2,1,0:T(8,128)(2,1)S(1)}, bf16[1,512,512]{2,1,0:T(8,128)(2,1)}, u32[]{:S(2)}) %copy-start.1) | copy-done | bytes 524312
  5.6 0.0 copy-start.2
  5.6 1.0 %copy-done.2 = bf16[1,512,512]{2,1,0:T(8,128)(2,1)S(1)} copy-done((bf16[1,512,512]{2,1,0:T(8,128)(2,1)S(1)}, bf16[1,512,512]{2,1,0:T(8,128)(2,1)}, u32[]{:S(2)}) %copy-start.2) | copy-done | bytes 524312
  6.7 0.0 copy-start.3
  6.7 0.7 copy-done.3
  7.3 0.0 copy-start.4
  7.3 0.7 copy-done.4
  8.0 0.0 copy-start.5
  8.0 0.7 copy-done.5
  8.6 0.0 copy-start.6
  8.6 0.7 copy-done.6
  9.3 92.7 %whole.1 = (f32[32,64,128]{2,1,0:T(8,128)S(1)}, f32[32,64,128]{2,1,0:T(8,128)S(1)}) custom-call(s32[64]{0:T(128)S(1)} %copy-done.3, s32[64]{0:T(128)S(1)} %copy-done.4, f32[64]{0:T(128)S(1)} %copy-done.5, s32[32]{0:T(128)S(1)} %copy-done.6, bf16[32,64,512]{2,1,0:T(8,128)(2,1)S(1)} %copy-done, f32[32,64,512]{2,1,0:T(8,128)} %diag_in.1, ...), custom_call_target="tpu_custom_call" | custom-call | tf_op jit(solution)/shard_map/whole/pallas_call | solution.py:311
  102.0 1.0 copy.10
  103.0 1.0 copy.11
Async XLA Ops:
  3.0 1.6 %copy-start = (bf16[32,64,512]{2,1,0:T(8,128)(2,1)S(1)}, bf16[32,64,512]{2,1,0:T(8,128)(2,1)}, u32[]{:S(2)}) copy-start(bf16[32,64,512]{2,1,0:T(8,128)(2,1)} %wave_in.1) | copy-start | bytes 6291460
  4.6 1.0 %copy-start.1 = (bf16[1,512,512]{2,1,0:T(8,128)(2,1)S(1)}, bf16[1,512,512]{2,1,0:T(8,128)(2,1)}, u32[]{:S(2)}) copy-start(bf16[1,512,512]{2,1,0:T(8,128)(2,1)} %left_in.1) | copy-start | bytes 1572868
  5.6 1.0 %copy-start.2 = (bf16[1,512,512]{2,1,0:T(8,128)(2,1)S(1)}, bf16[1,512,512]{2,1,0:T(8,128)(2,1)}, u32[]{:S(2)}) copy-start(bf16[1,512,512]{2,1,0:T(8,128)(2,1)} %right_in.1) | copy-start | bytes 1572868
  6.7 0.7 copy-start.3
  7.3 0.7 copy-start.4
  8.0 0.7 copy-start.5
  8.6 0.7 copy-start.6

commit v3 on v2

--- a/solution.py
+++ b/solution.py
@@ -82,10 +82,10 @@
 
             lax.fori_loop(1 if dg == 0 else 0, ops_count, step, 0)
 
-    def place(ref, side, at_o, at_g):
+    def place(ref, side, at_o, at_g, first=0, count=rows):
         return ref.at[
             side, :,
-            pl.ds(pl.multiple_of(at_o * rows, rows), rows),
+            pl.ds(pl.multiple_of(at_o * rows + first, count), count),
             pl.ds(pl.multiple_of(at_g * cols, cols), cols),
         ]
 
@@ -155,7 +155,7 @@
         square = value * value
         return carry[0] + fold(diag[k] * square), carry[1] + fold(square)
 
-    top, norm = lax.fori_loop(0, sectors, tally, (zero, zero))
+    top, norm = lax.fori_loop(0, sectors, tally, (zero, zero), unroll=2)
     loads[1].wait()
     loads[2].wait()
 
@@ -166,28 +166,56 @@
         whole_of(group, like).wait_send()
 
     fetch_like = [blocks_a.at[s, :, pl.ds(0, (ops_count - 1) * rows), :] for s in range(2)]
-    like_b = [pieces_b.at[s, pl.ds(0, (devices - 1) * pair_dev)] for s in range(2)]
-    like_c = [send_c.at[s, pl.ds(0, (devices - 1) * pair_dev)] for s in range(2)]
-    like_d = [pieces_d.at[s, pl.ds(0, (devices - 1) * pair_dev)] for s in range(2)]
+    others = pl.ds(0, (devices - 1) * pair_dev)
+    short = rows // 2
+    parts = [(h * short, short) for h in range(2)]
     stats_like = all_stats.at[pl.ds(0, devices - 1)]
     my_pairs = pl.ds(me * pair_dev, pair_dev)
-
-    def scatter(side, group, out, pieces):
+    first_b, first_c, first_d, stats_group = 2, 5, 9, 12
+
+    def cut(ref, side, which, part):
+        return ref.at[side, which, pl.ds(*part)]
+
+    def scatter(side, group, out, pieces, part):
         copy = pltpu.make_async_copy(
-            place(out, side, o, g), pieces.at[side, my_pairs], own_sem.at[group]
+            place(out, side, o, g, *part), cut(pieces, side, my_pairs, part), own_sem.at[group]
         )
         copy.start()
         each_peer(
             lambda to_o, to_g: send(
-                group, place(out, side, to_o, to_g), pieces.at[side, my_pairs], to_o, to_g
+                group, place(out, side, to_o, to_g, *part),
+                cut(pieces, side, my_pairs, part), to_o, to_g,
             )
         )
         return copy
 
+    def scatter_all(side, first_group, out, pieces):
+        if side == 0:
+            return [scatter(0, first_group, out, pieces, (0, rows))]
+        return [scatter(1, first_group + 1 + h, out, pieces, parts[h]) for h in range(2)]
+
+    def chain(pieces, side, part):
+        at = pl.ds(*part)
+
+        def visit(p, carry):
+            item = side * pairs + p
+            value = pieces[side, p, at].astype(wide)
+            run[item, at] = value + keep[item] * run[previous[item], at]
+            return carry
+
+        lax.fori_loop(0, pairs, visit, 0, unroll=4)
+
+    scattered = []
     for side in range(2):
         arrive(fetch_groups[side], fetch_like[side])
         own[side].wait()
-        if side == 1:
+        if side == 0:
+            out_f = []
+            for j in range(pair_dev):
+                value = product(0, left[j], right[j], blocks_a[0, j])
+                out_b[0, j] = value.astype(jnp.bfloat16)
+                out_f.append(value)
+        else:
             for j in range(pair_dev):
                 value = product(1, left[j], right[j], blocks_a[1, j])
                 out_b[1, j] = value.astype(jnp.bfloat16)
@@ -195,96 +223,98 @@
                 top = top + fold(blocks_a[1, j].astype(wide) * out_f[j])
             stats[0] = top
             stats[1] = norm
-            own.append(pltpu.make_async_copy(stats, all_stats.at[me], own_sem.at[8]))
-            own[-1].start()
-            each_peer(lambda to_o, to_g: send(8, stats, all_stats.at[me], to_o, to_g))
-        else:
-            out_f = []
-            for j in range(pair_dev):
-                value = product(0, left[j], right[j], blocks_a[0, j])
-                out_b[0, j] = value.astype(jnp.bfloat16)
-                out_f.append(value)
-        own.append(scatter(side, 2 + side, out_b, pieces_b))
-
-    def chain(pieces):
-        for side in range(2):
-
-            def visit(p, carry, side=side):
-                item = side * pairs + p
-                run[item] = pieces[side, p].astype(wide) + keep[item] * run[previous[item]]
-                return carry
-
-            lax.fori_loop(0, pairs, visit, 0)
-
-    for copy in own[2:]:
-        copy.wait()
-    for side in range(2):
-        arrive(2 + side, like_b[side])
-    arrive(8, stats_like)
+            own_stats = pltpu.make_async_copy(stats, all_stats.at[me], own_sem.at[stats_group])
+            own_stats.start()
+            each_peer(lambda to_o, to_g: send(stats_group, stats, all_stats.at[me], to_o, to_g))
+        scattered += scatter_all(side, first_b, out_b, pieces_b)
+
+    scattered[0].wait()
+    arrive(first_b, cut(pieces_b, 0, others, (0, rows)))
     run[0] = jnp.zeros((rows, cols), wide)
-    chain(pieces_b)
+    chain(pieces_b, 0, (0, rows))
+    own_stats.wait()
+    arrive(stats_group, stats_like)
     sums = jnp.sum(all_stats[...], axis=0)
     rayleigh = jnp.sum(sums[0]) / jnp.sum(sums[1])
 
-    def finish(k, carry):
-        value = (diag[k] - rayleigh) * wave[k, :, my_cols].astype(wide) + run[last[k]]
-        residual[k] = value
-        half[k] = value.astype(jnp.bfloat16)
-        return carry
-
-    lax.fori_loop(0, sectors, finish, 0)
+    returned = {}
+    for h, part in enumerate(parts):
+        scattered[1 + h].wait()
+        arrive(first_b + 1 + h, cut(pieces_b, 1, others, part))
+        chain(pieces_b, 1, part)
+        at = pl.ds(*part)
+
+        def finish(k, carry, at=at):
+            value = (diag[k, at] - rayleigh) * wave[k, at, my_cols].astype(wide)
+            value = value + run[last[k], at]
+            residual[k, at] = value
+            half[k, at] = value.astype(jnp.bfloat16)
+            return carry
+
+        lax.fori_loop(0, sectors, finish, 0, unroll=4)
+        for side in range(2):
+            group = first_c + 2 * h + side
+
+            def hand_out(p, carry, side=side, at=at):
+                send_c[side, p, at] = half[slots[side * pairs + p], at]
+                return carry
+
+            lax.fori_loop(0, pairs, hand_out, 0, unroll=8)
+            target = place(blocks_c, side, o, g, *part)
+
+            def collect(to_o, to_g, side=side, group=group, part=part, target=target):
+                to = to_o * grp_count + to_g
+                which = pl.ds(to * pair_dev, pair_dev)
+                send(group, cut(send_c, side, which, part), target, to_o, to_g)
+
+            each_peer(collect)
+            returned[side, h] = pltpu.make_async_copy(
+                cut(send_c, side, my_pairs, part), target, own_sem.at[group]
+            )
+            returned[side, h].start()
     residual_copy = pltpu.make_async_copy(residual, residual_out, load_sem.at[0])
     residual_copy.start()
-
-    own = []
+    scattered = []
     for side in range(2):
-
-        def hand_out(p, carry, side=side):
-            send_c[side, p] = half[slots[side * pairs + p]]
-            return carry
-
-        lax.fori_loop(0, pairs, hand_out, 0)
-
-        def collect(to_o, to_g, side=side):
-            to = to_o * grp_count + to_g
-            source = send_c.at[side, pl.ds(to * pair_dev, pair_dev)]
-            send(4 + side, source, place(blocks_c, side, o, g), to_o, to_g)
-
-        each_peer(collect)
-        own.append(
-            pltpu.make_async_copy(
-                send_c.at[side, my_pairs], place(blocks_c, side, o, g), own_sem.at[4 + side]
-            )
-        )
-        own[side].start()
-    for side in range(2):
-        own[side].wait()
-        arrive(4 + side, like_c[side])
+        for h, part in enumerate(parts):
+            returned[side, h].wait()
+            arrive(first_c + 2 * h + side, cut(send_c, side, others, part))
         for j in range(pair_dev):
             value = product(side, left[j], right[j], blocks_c[side, j])
             out_d[side, j] = value.astype(jnp.bfloat16)
-        own.append(scatter(side, 6 + side, out_d, pieces_d))
-    for side in range(2):
-        own[2 + side].wait()
-        arrive(6 + side, like_d[side])
+        scattered += scatter_all(side, first_d, out_d, pieces_d)
+    scattered[0].wait()
+    arrive(first_d, cut(pieces_d, 0, others, (0, rows)))
     run[0] = jnp.zeros((rows, cols), wide)
-    chain(pieces_d)
-
-    def close(k, carry):
-        sigma[k] = diag[k] * half[k].astype(wide) + run[last[k]]
-        return carry
-
-    lax.fori_loop(0, sectors, close, 0)
-    sigma_copy = pltpu.make_async_copy(sigma, sigma_out, load_sem.at[1])
-    sigma_copy.start()
+    chain(pieces_d, 0, (0, rows))
+    sigma_copies = []
+    for h, part in enumerate(parts):
+        scattered[1 + h].wait()
+        arrive(first_d + 1 + h, cut(pieces_d, 1, others, part))
+        chain(pieces_d, 1, part)
+        at = pl.ds(*part)
+
+        def close(k, carry, at=at):
+            sigma[k, at] = diag[k, at] * half[k, at].astype(wide) + run[last[k], at]
+            return carry
+
+        lax.fori_loop(0, sectors, close, 0, unroll=4)
+        copy = pltpu.make_async_copy(sigma.at[:, at], sigma_out.at[:, at], load_sem.at[1 + h])
+        copy.start()
+        sigma_copies.append(copy)
     for side in range(2):
         leave(side, fetch_like[side])
-        leave(2 + side, like_b[side])
-        leave(4 + side, like_c[side])
-        leave(6 + side, like_d[side])
-    leave(8, stats_like)
+    for first, pieces in ((first_b, pieces_b), (first_d, pieces_d)):
+        leave(first, cut(pieces, 0, others, (0, rows)))
+        for h, part in enumerate(parts):
+            leave(first + 1 + h, cut(pieces, 1, others, part))
+    for h, part in enumerate(parts):
+        for side in range(2):
+            leave(first_c + 2 * h + side, cut(send_c, side, others, part))
+    leave(stats_group, stats_like)
     residual_copy.wait()
-    sigma_copy.wait()
+    for copy in sigma_copies:
+        copy.wait()
 
 
 def direct_body(wave, diag_energy, left_ops, right_ops, pair_sectors, sector_slot):
@@ -322,11 +352,11 @@
             pltpu.VMEM((2 * pairs, rows, cols), wide), pltpu.VMEM(share, wide),
             pltpu.VMEM(share, thin), pltpu.VMEM(share, wide),
             pltpu.VMEM((2, 8, 128), wide), pltpu.VMEM((devices, 2, 8, 128), wide),
-            pltpu.SemaphoreType.DMA((4,)), pltpu.SemaphoreType.DMA((9,)),
-            pltpu.SemaphoreType.DMA((9,)), pltpu.SemaphoreType.DMA((9,)),
+            pltpu.SemaphoreType.DMA((4,)), pltpu.SemaphoreType.DMA((13,)),
+            pltpu.SemaphoreType.DMA((13,)), pltpu.SemaphoreType.DMA((13,)),
         ],
         compiler_params=pltpu.CompilerParams(
-            collective_id=0, has_side_effects=True, vmem_limit_bytes=48 << 20
+            collective_id=0, has_side_effects=True, vmem_limit_bytes=63 << 20
         ),
     )(*chains, wave, diag_energy, left_ops, right_ops)
 
@@ -409,7 +439,7 @@
 
 
 def solution(mesh):
-    rows_tile, lane_tile, most_peers = 16, 128, 64
+    rows_tile, lane_tile, most_peers = 32, 128, 64
 
     def body(wave, diag_energy, left_ops, right_ops, pair_sectors, sector_slot):
         rows, width = wave.shape[1:]

time: 104 us -> 99.3 us (0.955)
  local copies, waits for them, and re-layouts: 8.24 us -> 4.61 us
  Pallas kernels: 95 us -> 93 us
    unnamed x16 -> x2, local copies, waits for them, and re-layouts: 8.24 us -> 4.61 us
    pallas_call x1, Pallas kernels: 92.7 us -> 90.6 us  [direct_body(): pl.pallas_call(functools.partial(whole_kernel, ops_count, grp_count, pair...]
where the time goes in v3:
time: 99.3 us; the launch traced here: 98.2 us
  Pallas kernels  93 us (94%)
  local copies, waits for them, and re-layouts  4.61 us (5%)
    pallas_call x1, Pallas kernels, direct_body(): pl.pallas_call(functools.partial(whole_kernel, ops_count, grp_count, pair...  90.6 us
    unnamed x2, local copies, waits for them, and re-layouts  4.61 us
    pallas_call x1, Pallas kernels, direct_body(): pl.pallas_call(chain_kernel, out_shape=(shape((2 * pairs,), jnp.int32), s...  2.34 us

profile of v3, /device:TPU:9, one launch (start us, length us, event | category | flops | bytes accessed | tf_op | source)
XLA Modules:
  0.0 98.2 jit_solution(3537512434817900795)
XLA Ops:
  0.6 2.3 %chain.1 = (s32[64]{0:T(128)}, s32[64]{0:T(128)}, f32[64]{0:T(128)}, s32[32]{0:T(128)}) custom-call(s32[2,32]{1,0:T(2,128)} %bitcast.1, s32[32]{0:T(128)} %sector_slot.1), custom_call_target="tpu_custom_call" | custom-call | tf_op jit(solution)/shard_map/chain/pallas_call | solution.py:330
  3.0 90.6 %whole.1 = (f32[32,64,128]{2,1,0:T(8,128)}, f32[32,64,128]{2,1,0:T(8,128)}) custom-call(s32[64]{0:T(128)} %get-tuple-element.6.slots, s32[64]{0:T(128)} %get-tuple-element.7.previous, f32[64]{0:T(128)} %get-tuple-element.8.keep, s32[32]{0:T(128)} %get-tuple-element.9.last, bf16[32,64,512]{2,1,0:T(8,128)(2,1)} %wave_in.1, f32[32,64,512]{2,1,0:T(8,128)} %diag_in.1, ...), custom_call_target="tpu_custom_call" | custom-call | tf_op jit(solution)/shard_map/whole/pallas_call | solution.py:341
  93.6 2.3 %copy.10 = f32[32,64,128]{2,1,0:T(8,128)} copy(f32[32,64,128]{2,1,0:T(8,128)} %get-tuple-element.12) | data formatting | bytes 2097152
  95.9 2.3 %copy.11 = f32[32,64,128]{2,1,0:T(8,128)} copy(f32[32,64,128]{2,1,0:T(8,128)} %get-tuple-element.13) | data formatting | bytes 2097152

commit v4 on v3

--- a/solution.py
+++ b/solution.py
@@ -11,30 +11,6 @@
 VMEM = pl.BlockSpec(memory_space=pltpu.VMEM)
 SMEM = pl.BlockSpec(memory_space=pltpu.SMEM)
 ANY = pl.BlockSpec(memory_space=pl.ANY)
-
-
-def chain_kernel(pair_sides, sector_slot, slots, previous, keep, last):
-    pairs = pair_sides.shape[1]
-    sectors = sector_slot.shape[0]
-
-    def clear(k, carry):
-        last[k] = -1
-        return carry
-
-    lax.fori_loop(0, sectors, clear, 0)
-    for side in range(2):
-
-        def visit(p, carry, side=side):
-            item = side * pairs + p
-            slots[item] = sector_slot[pair_sides[side, p]]
-            k = sector_slot[pair_sides[1 - side, p]]
-            before = last[k]
-            previous[item] = jnp.maximum(before, 0)
-            keep[item] = jnp.where(before >= 0, 1.0, 0.0)
-            last[k] = item
-            return carry
-
-        lax.fori_loop(0, pairs, visit, 0)
 
 
 def fold(value):
@@ -57,11 +33,11 @@
 
 def whole_kernel(
     ops_count, grp_count, pair_dev,
-    slots, previous, keep, last, wave_in, diag_in, left_in, right_in,
+    pair_sides, sector_slot, wave_in, diag_in, left_in, right_in,
     residual_out, sigma_out,
     wave, diag, left, right, send_a, blocks_a, out_b, pieces_b, send_c, blocks_c,
     out_d, pieces_d, run, residual, half, sigma, stats, all_stats,
-    load_sem, own_sem, send_sem, recv_sem,
+    load_sem, own_sem, send_sem, recv_sem, slots, keys, previous, keep, last,
 ):
     o, g = lax.axis_index("ops"), lax.axis_index("grp")
     me = o * grp_count + g
@@ -118,6 +94,15 @@
         )
     )
 
+    for side in range(2):
+
+        def name(p, carry, side=side):
+            slots[side * pairs + p] = sector_slot[pair_sides[side, p]]
+            keys[side * pairs + p] = sector_slot[pair_sides[1 - side, p]]
+            return carry
+
+        lax.fori_loop(0, pairs, name, 0, unroll=4)
+
     loads[0].wait()
 
     def stage(side):
@@ -127,14 +112,10 @@
                 send_a[side, to, j] = wave[slots[side * pairs + pair]]
 
     fetch_groups, own = (0, 1), []
-    stage(0)
-    pl.semaphore_wait(barrier, devices - 1)
     my_rows = pl.ds(pl.multiple_of(o * rows, rows), rows)
-    for side in range(2):
-        if side == 1:
-            stage(1)
-
-        def fetch(do, carry, side=side):
+
+    def fetch_side(side):
+        def fetch(do, carry):
             to = lax.rem(o + do, ops_count)
             send(fetch_groups[side], send_a.at[side, to], blocks_a.at[side, :, my_rows, :], to, g)
             return carry
@@ -146,6 +127,11 @@
             )
         )
         own[side].start()
+
+    stage(0)
+    pl.semaphore_wait(barrier, devices - 1)
+    fetch_side(0)
+    stage(1)
 
     loads[3].wait()
     zero = jnp.zeros((8, 128), wide)
@@ -206,6 +192,8 @@
         lax.fori_loop(0, pairs, visit, 0, unroll=4)
 
     scattered = []
+    leave(0, fetch_like[0])
+    fetch_side(1)
     for side in range(2):
         arrive(fetch_groups[side], fetch_like[side])
         own[side].wait()
@@ -228,6 +216,30 @@
             each_peer(lambda to_o, to_g: send(stats_group, stats, all_stats.at[me], to_o, to_g))
         scattered += scatter_all(side, first_b, out_b, pieces_b)
 
+    for side in range(2):
+
+        def link(p, carry, side=side):
+            item = side * pairs + p
+            key = keys[item]
+
+            def look(other, found):
+                return jnp.where((keys[other] == key) & (other < item), other, found)
+
+            before = lax.fori_loop(0, (side + 1) * pairs, look, -1, unroll=16)
+            previous[item] = jnp.maximum(before, 0)
+            keep[item] = jnp.where(before >= 0, 1.0, 0.0)
+            return carry
+
+        lax.fori_loop(0, pairs, link, 0)
+
+    def close_chain(k, carry):
+        def look(other, found):
+            return jnp.where(keys[other] == k, other, found)
+
+        last[k] = lax.fori_loop(0, 2 * pairs, look, 0, unroll=16)
+        return carry
+
+    lax.fori_loop(0, sectors, close_chain, 0)
     scattered[0].wait()
     arrive(first_b, cut(pieces_b, 0, others, (0, rows)))
     run[0] = jnp.zeros((rows, cols), wide)
@@ -302,8 +314,7 @@
         copy = pltpu.make_async_copy(sigma.at[:, at], sigma_out.at[:, at], load_sem.at[1 + h])
         copy.start()
         sigma_copies.append(copy)
-    for side in range(2):
-        leave(side, fetch_like[side])
+    leave(1, fetch_like[1])
     for first, pieces in ((first_b, pieces_b), (first_d, pieces_d)):
         leave(first, cut(pieces, 0, others, (0, rows)))
         for h, part in enumerate(parts):
@@ -327,21 +338,13 @@
     devices = ops_count * grp_count
     thin, wide = jnp.bfloat16, jnp.float32
     shape = jax.ShapeDtypeStruct
-    chains = pl.pallas_call(
-        chain_kernel,
-        out_shape=(
-            shape((2 * pairs,), jnp.int32), shape((2 * pairs,), jnp.int32),
-            shape((2 * pairs,), wide), shape((sectors,), jnp.int32),
-        ),
-        in_specs=[SMEM, SMEM], out_specs=(SMEM,) * 4, name="chain",
-    )(pair_sectors.T, sector_slot)
     blocks = (2, pair_dev, height, width)
     pieces = (2, pairs, rows, cols)
     share = (sectors, rows, cols)
     return pl.pallas_call(
         functools.partial(whole_kernel, ops_count, grp_count, pair_dev),
         out_shape=(shape(share, wide), shape(share, wide)),
-        in_specs=[SMEM] * 4 + [ANY] * 4, out_specs=(ANY, ANY), name="whole",
+        in_specs=[SMEM] * 2 + [ANY] * 4, out_specs=(ANY, ANY), name="whole",
         scratch_shapes=[
             pltpu.VMEM(wave.shape, thin), pltpu.VMEM(share, wide),
             pltpu.VMEM(left_ops.shape, thin), pltpu.VMEM(right_ops.shape, thin),
@@ -354,11 +357,14 @@
             pltpu.VMEM((2, 8, 128), wide), pltpu.VMEM((devices, 2, 8, 128), wide),
             pltpu.SemaphoreType.DMA((4,)), pltpu.SemaphoreType.DMA((13,)),
             pltpu.SemaphoreType.DMA((13,)), pltpu.SemaphoreType.DMA((13,)),
+            pltpu.SMEM((2 * pairs,), jnp.int32), pltpu.SMEM((2 * pairs,), jnp.int32),
+            pltpu.SMEM((2 * pairs,), jnp.int32), pltpu.SMEM((2 * pairs,), wide),
+            pltpu.SMEM((sectors,), jnp.int32),
         ],
         compiler_params=pltpu.CompilerParams(
             collective_id=0, has_side_effects=True, vmem_limit_bytes=63 << 20
         ),
-    )(*chains, wave, diag_energy, left_ops, right_ops)
+    )(pair_sectors.T, sector_slot, wave, diag_energy, left_ops, right_ops)
 
 
 def segment_total(received, targets, sectors):

time: 99.3 us -> 96.6 us (0.973)
  Pallas kernels: 93 us -> 90.3 us
    pallas_call x1 -> x0, Pallas kernels: 2.34 us -> none  [direct_body(): pl.pallas_call(chain_kernel, out_shape=(shape((2 * pairs,), jnp.int32), s...]
where the time goes in v4:
time: 96.6 us; the launch traced here: 95.6 us
  Pallas kernels  90.3 us (93%)
  local copies, waits for them, and re-layouts  4.61 us (5%)
    pallas_call x1, Pallas kernels, direct_body(): pl.pallas_call(functools.partial(whole_kernel, ops_count, grp_count, pair...  90.3 us
    unnamed x2, local copies, waits for them, and re-layouts  4.61 us

profile of v4, /device:TPU:9, one launch (start us, length us, event | category | flops | bytes accessed | tf_op | source)
XLA Modules:
  0.0 95.6 jit_solution(12167646180866037921)
XLA Ops:
  0.6 90.3 %whole.1 = (f32[32,64,128]{2,1,0:T(8,128)}, f32[32,64,128]{2,1,0:T(8,128)}) custom-call(s32[2,32]{1,0:T(2,128)} %bitcast.1, s32[32]{0:T(128)} %sector_slot.1, bf16[32,64,512]{2,1,0:T(8,128)(2,1)} %wave_in.1, f32[32,64,512]{2,1,0:T(8,128)} %diag_in.1, bf16[1,512,512]{2,1,0:T(8,128)(2,1)} %left_in.1, bf16[1,512,512]{2,1,0:T(8,128)(2,1)} %right_in.1), custom_call_target="tpu_custom_call" | custom-call | tf_op jit(solution)/shard_map/whole/pallas_call | solution.py:344
  91.0 2.3 %copy.10 = f32[32,64,128]{2,1,0:T(8,128)} copy(f32[32,64,128]{2,1,0:T(8,128)} %get-tuple-element.4) | data formatting | bytes 2097152
  93.3 2.3 %copy.11 = f32[32,64,128]{2,1,0:T(8,128)} copy(f32[32,64,128]{2,1,0:T(8,128)} %get-tuple-element.5) | data formatting | bytes 2097152
